TPU v7x, 512 devices: a whole 4x8x8 slice. The times are simulated.
512 devices in a mesh: skill: 64 (over y_lo, x, z), tensor: 8 (over y_hi, core).
Axes of the slice: x: 4, y: 8 (y_hi: 4, y_lo: 2; y = y_hi * 2 + y_lo), z: 8, core: 2. Of those that a mesh axis runs over, the one named last changes fastest.
Arguments:
- stored_inputs: bfloat16 [64, 256, 8192], P('skill', None, 'tensor'), may hold values from -6 to 6
- stored_output_gradient: bfloat16 [64, 256, 15360], P('skill', None, 'tensor'), may hold values from -6 to 6
- training_token_index: int32 [64, 256], P('skill'), may hold values from 0 to 255
- validation_inputs: bfloat16 [64, 512, 8192], P('skill', None, 'tensor'), may hold values from -6 to 6
- validation_output_gradient: bfloat16 [64, 512, 15360], P('skill', None, 'tensor'), may hold values from -6 to 6
- validation_row_skill: int32 [64, 512], P('skill'), may hold values from 0 to 63
- adapter_down_init: bfloat16 [64, 8192, 64], P('skill', 'tensor'), may hold values from -0.0625 to 0.0625
Outputs:
- own_delta: float32 [64, 17], P('skill')
- other_delta: float32 [64, 17], P('skill')
All inputs are finite; a program needn't handle non-finite values.
Results may differ from a plain program's by a relative error of at most 0.0042.
Values may be sent and summed in bfloat16 or wider, within the bound.
A program may use at most 64 MiB of HBM per device.

v0:
```python
import jax
import jax.numpy as jnp
from jax import lax
from jax.sharding import PartitionSpec as P


def from_behind(block, axis, distance):
    devices = range(lax.axis_size(axis))
    route = [((i - distance) % len(devices), i) for i in devices]
    return lax.ppermute(block, axis, route)


def evaluate(down_piece, up_piece, valid_act, valid_cot, own_mask, other_mask):
    partial_value = jnp.dot(valid_act, down_piece, preferred_element_type=jnp.float32)
    summed = lax.psum(partial_value, "tensor")
    cot_proj = lax.dot_general(
        valid_cot, up_piece, (((1,), (1,)), ((), ())), preferred_element_type=jnp.float32
    )
    row_change = jnp.sum(summed * cot_proj, axis=1)
    return jnp.stack([jnp.sum(row_change * own_mask), jnp.sum(row_change * other_mask)])


def on_device(
    stored_inputs,
    stored_output_gradient,
    training_token_index,
    validation_inputs,
    validation_output_gradient,
    validation_row_skill,
    adapter_down_init,
):
    chosen = training_token_index[0]
    train_act = jnp.take(stored_inputs[0], chosen, axis=0)
    train_cot = jnp.take(stored_output_gradient[0], chosen, axis=0)
    local_down_factor = adapter_down_init[0]
    partial_value = jnp.dot(train_act, local_down_factor, preferred_element_type=jnp.float32)
    proj = lax.psum(partial_value, "tensor").astype(jnp.bfloat16)
    product = lax.dot_general(
        proj, train_cot, (((0,), (0,)), ((), ())), preferred_element_type=jnp.float32
    )
    up_local = (product * (-1.0 / chosen.shape[0])).astype(jnp.bfloat16)
    valid_act = validation_inputs[0]
    valid_cot = validation_output_gradient[0]
    labels = validation_row_skill[0]
    my_skill = lax.axis_index("skill")
    own_mask = (labels == my_skill).astype(jnp.float32)
    other_mask = 1.0 - own_mask

    def score(down_piece, up_piece):
        return evaluate(down_piece, up_piece, valid_act, valid_cot, own_mask, other_mask)

    reach_count = lax.axis_size("skill") // 8
    column_count = 2 * reach_count + 1
    scores = jnp.zeros((column_count, 2), jnp.float32)
    first_down, first_up = from_behind((local_down_factor, up_local), "skill", reach_count)

    def advance(column, carry):
        held_down, held_up, table = carry
        table = table.at[column].set(score(held_down, held_up))
        held_down, held_up = from_behind((held_down, held_up), "skill", -1)
        return (held_down, held_up, table)

    last_down, last_up, scores = lax.fori_loop(
        0, column_count - 1, advance, (first_down, first_up, scores)
    )
    scores = scores.at[column_count - 1].set(score(last_down, last_up))
    totals = lax.psum(scores, "tensor")
    own_count = jnp.maximum(jnp.sum(own_mask), 1.0)
    other_count = jnp.maximum(jnp.sum(other_mask), 1.0)
    own_delta = (totals[:, 0] / own_count)[None, :]
    other_delta = (totals[:, 1] / other_count)[None, :]
    return (own_delta, other_delta)


def solution(mesh):
    in_specs = (
        P("skill", None, "tensor"),
        P("skill", None, "tensor"),
        P("skill", None),
        P("skill", None, "tensor"),
        P("skill", None, "tensor"),
        P("skill", None),
        P("skill", "tensor", None),
    )
    out_specs = (P("skill", None), P("skill", None))
    return jax.shard_map(
        on_device, mesh=mesh, in_specs=in_specs, out_specs=out_specs, check_vma=False
    )
```

profile of v0, /device:TPU:2, one launch (start us, length us, event | category | flops | bytes accessed | tf_op | source)
XLA Modules:
  0.0 1527.6 jit_solution(34875046202805492)
XLA Ops:
  12.5 32.0 %psum.32 = bf16[256,64]{1,0:T(8,128)(2,1)S(1)} all-reduce(f32[256,64]{1,0:T(8,128)S(1)} %fusion.4), channel_id=1, replica_groups=mesh['skill'=64,'tensor'=8] {'tensor'}, use_global_device_ids=true, to_apply=%region_0.1 | all-reduce | flops 16384 | bytes 98304 | tf_op jit(solution)/shard_map/psum | solution.py:37
  55.9 6.8 collective-permute-done.2
  62.7 1346.3 %while.19 = (s32[]{:T(128)}, bf16[1024,64]{1,0:T(8,128)(2,1)}, bf16[64,1920]{1,0:T(8,128)(2,1)}, f32[17,2]{1,0:T(8,128)S(1)}, bf16[512,1024]{1,0:T(8,128)(2,1)},...) while((s32[]{:T(128)}, bf16[1024,64]{1,0:T(8,128)(2,1)}, ...), condition=%wide.region_7.8_spmd, body=%wide.region_1.7_spmd.sunk | while | flops 193037824 | bytes 6709567 | solution.py:63
  66.0 11.7 collective-permute-start
  81.8 63.7 %all-reduce.5.cloned.1.call-done = f32[512,64]{0,1:T(8,128)} async-done(((f32[512,64]{0,1:T(8,128)}), f32[512,64]{0,1:T(8,128)}) %all-reduce.5.cloned.1.call-update) | async-done | bytes 131088 | tf_op jit(solution)/shard_map/while/body/eval_jaxpr/psum | solution.py:15
  153.1 5.9 collective-permute-start
  163.8 65.9 %all-reduce.5.cloned.1.call-done = f32[512,64]{0,1:T(8,128)} async-done(((f32[512,64]{0,1:T(8,128)}), f32[512,64]{0,1:T(8,128)}) %all-reduce.5.cloned.1.call-update) | async-done | bytes 131088 | tf_op jit(solution)/shard_map/while/body/eval_jaxpr/psum | solution.py:15
  237.3 5.9 collective-permute-start
  248.0 65.9 %all-reduce.5.cloned.1.call-done = f32[512,64]{0,1:T(8,128)} async-done(((f32[512,64]{0,1:T(8,128)}), f32[512,64]{0,1:T(8,128)}) %all-reduce.5.cloned.1.call-update) | async-done | bytes 131088 | tf_op jit(solution)/shard_map/while/body/eval_jaxpr/psum | solution.py:15
  332.1 65.5 %all-reduce.5.cloned.1.call-done = f32[512,64]{0,1:T(8,128)} async-done(((f32[512,64]{0,1:T(8,128)}), f32[512,64]{0,1:T(8,128)}) %all-reduce.5.cloned.1.call-update) | async-done | bytes 131088 | tf_op jit(solution)/shard_map/while/body/eval_jaxpr/psum | solution.py:15
  415.9 65.5 %all-reduce.5.cloned.1.call-done = f32[512,64]{0,1:T(8,128)} async-done(((f32[512,64]{0,1:T(8,128)}), f32[512,64]{0,1:T(8,128)}) %all-reduce.5.cloned.1.call-update) | async-done | bytes 131088 | tf_op jit(solution)/shard_map/while/body/eval_jaxpr/psum | solution.py:15
  499.7 65.5 %all-reduce.5.cloned.1.call-done = f32[512,64]{0,1:T(8,128)} async-done(((f32[512,64]{0,1:T(8,128)}), f32[512,64]{0,1:T(8,128)}) %all-reduce.5.cloned.1.call-update) | async-done | bytes 131088 | tf_op jit(solution)/shard_map/while/body/eval_jaxpr/psum | solution.py:15
  583.5 65.8 %all-reduce.5.cloned.1.call-done = f32[512,64]{0,1:T(8,128)} async-done(((f32[512,64]{0,1:T(8,128)}), f32[512,64]{0,1:T(8,128)}) %all-reduce.5.cloned.1.call-update) | async-done | bytes 131088 | tf_op jit(solution)/shard_map/while/body/eval_jaxpr/psum | solution.py:15
  667.6 65.8 %all-reduce.5.cloned.1.call-done = f32[512,64]{0,1:T(8,128)} async-done(((f32[512,64]{0,1:T(8,128)}), f32[512,64]{0,1:T(8,128)}) %all-reduce.5.cloned.1.call-update) | async-done | bytes 131088 | tf_op jit(solution)/shard_map/while/body/eval_jaxpr/psum | solution.py:15
  751.7 65.8 %all-reduce.5.cloned.1.call-done = f32[512,64]{0,1:T(8,128)} async-done(((f32[512,64]{0,1:T(8,128)}), f32[512,64]{0,1:T(8,128)}) %all-reduce.5.cloned.1.call-update) | async-done | bytes 131088 | tf_op jit(solution)/shard_map/while/body/eval_jaxpr/psum | solution.py:15
  835.8 65.6 %all-reduce.5.cloned.1.call-done = f32[512,64]{0,1:T(8,128)} async-done(((f32[512,64]{0,1:T(8,128)}), f32[512,64]{0,1:T(8,128)}) %all-reduce.5.cloned.1.call-update) | async-done | bytes 131088 | tf_op jit(solution)/shard_map/while/body/eval_jaxpr/psum | solution.py:15
  919.6 65.8 %all-reduce.5.cloned.1.call-done = f32[512,64]{0,1:T(8,128)} async-done(((f32[512,64]{0,1:T(8,128)}), f32[512,64]{0,1:T(8,128)}) %all-reduce.5.cloned.1.call-update) | async-done | bytes 131088 | tf_op jit(solution)/shard_map/while/body/eval_jaxpr/psum | solution.py:15
  1003.7 65.5 %all-reduce.5.cloned.1.call-done = f32[512,64]{0,1:T(8,128)} async-done(((f32[512,64]{0,1:T(8,128)}), f32[512,64]{0,1:T(8,128)}) %all-reduce.5.cloned.1.call-update) | async-done | bytes 131088 | tf_op jit(solution)/shard_map/while/body/eval_jaxpr/psum | solution.py:15
  1087.5 65.8 %all-reduce.5.cloned.1.call-done = f32[512,64]{0,1:T(8,128)} async-done(((f32[512,64]{0,1:T(8,128)}), f32[512,64]{0,1:T(8,128)}) %all-reduce.5.cloned.1.call-update) | async-done | bytes 131088 | tf_op jit(solution)/shard_map/while/body/eval_jaxpr/psum | solution.py:15
  1171.6 65.5 %all-reduce.5.cloned.1.call-done = f32[512,64]{0,1:T(8,128)} async-done(((f32[512,64]{0,1:T(8,128)}), f32[512,64]{0,1:T(8,128)}) %all-reduce.5.cloned.1.call-update) | async-done | bytes 131088 | tf_op jit(solution)/shard_map/while/body/eval_jaxpr/psum | solution.py:15
  1255.4 65.6 %all-reduce.5.cloned.1.call-done = f32[512,64]{0,1:T(8,128)} async-done(((f32[512,64]{0,1:T(8,128)}), f32[512,64]{0,1:T(8,128)}) %all-reduce.5.cloned.1.call-update) | async-done | bytes 131088 | tf_op jit(solution)/shard_map/while/body/eval_jaxpr/psum | solution.py:15
  1339.2 65.5 %all-reduce.5.cloned.1.call-done = f32[512,64]{0,1:T(8,128)} async-done(((f32[512,64]{0,1:T(8,128)}), f32[512,64]{0,1:T(8,128)}) %all-reduce.5.cloned.1.call-update) | async-done | bytes 131088 | tf_op jit(solution)/shard_map/while/body/eval_jaxpr/psum | solution.py:15
  1413.1 74.8 %all-reduce.3.cloned.1.call-done = f32[512,64]{0,1:T(8,128)} async-done(((f32[512,64]{0,1:T(8,128)}), f32[512,64]{0,1:T(8,128)}) %all-reduce.3.cloned.1.call-update) | async-done | bytes 131088 | tf_op jit(solution)/shard_map/psum | solution.py:15
  1490.9 27.6 %psum.34 = f32[17,2]{1,0:T(8,128)S(1)} all-reduce(f32[17,2]{1,0:T(8,128)S(1)} %scatter.7), channel_id=1, replica_groups=mesh['skill'=64,'tensor'=8] {'tensor'}, use_global_device_ids=true, to_apply=%region_12.13 | all-reduce | flops 34 | bytes 272 | tf_op jit(solution)/shard_map/psum | solution.py:67
  (255 shorter events, 297.2 us)
Async XLA Ops:
  62.7 82.8 %all-reduce.5.cloned.1.call-start = ((), (), s32[]{:S(2)}) async-start(), calls=%async_computation.1 | async-start | bytes 262144 | tf_op jit(solution)/shard_map/while/body/eval_jaxpr/psum | solution.py:15
  66.0 83.7 %collective-permute-start = (bf16[1024,64]{1,0:T(8,128)(2,1)S(1)}, bf16[1024,64]{1,0:T(8,128)(2,1)}, u32[]{:S(2)}, u32[]{:S(2)}) collective-permute-start(bf16[1024,64]{1,0:T(8,128)(2,1)S(1)} %copy.18), channel_id=1, source_target_pairs={{8,0},{16,8},{24,16},{32,24},{40,32},{48,40},{56,48},{64,56},{72,6... | collective-permute-start | bytes 393224 | tf_op jit(solution)/shard_map/while/body/eval_jaxpr/ppermute | solution.py:10
  149.8 79.9 %all-reduce.5.cloned.1.call-start = ((), (), s32[]{:S(2)}) async-start(), calls=%async_computation.1 | async-start | bytes 262144 | tf_op jit(solution)/shard_map/while/body/eval_jaxpr/psum | solution.py:15
  153.1 80.8 %collective-permute-start = (bf16[1024,64]{1,0:T(8,128)(2,1)S(1)}, bf16[1024,64]{1,0:T(8,128)(2,1)}, u32[]{:S(2)}, u32[]{:S(2)}) collective-permute-start(bf16[1024,64]{1,0:T(8,128)(2,1)S(1)} %copy.18), channel_id=1, source_target_pairs={{8,0},{16,8},{24,16},{32,24},{40,32},{48,40},{56,48},{64,56},{72,6... | collective-permute-start | bytes 393224 | tf_op jit(solution)/shard_map/while/body/eval_jaxpr/ppermute | solution.py:10
  233.9 79.9 %all-reduce.5.cloned.1.call-start = ((), (), s32[]{:S(2)}) async-start(), calls=%async_computation.1 | async-start | bytes 262144 | tf_op jit(solution)/shard_map/while/body/eval_jaxpr/psum | solution.py:15
  237.3 80.8 %collective-permute-start = (bf16[1024,64]{1,0:T(8,128)(2,1)S(1)}, bf16[1024,64]{1,0:T(8,128)(2,1)}, u32[]{:S(2)}, u32[]{:S(2)}) collective-permute-start(bf16[1024,64]{1,0:T(8,128)(2,1)S(1)} %copy.18), channel_id=1, source_target_pairs={{8,0},{16,8},{24,16},{32,24},{40,32},{48,40},{56,48},{64,56},{72,6... | collective-permute-start | bytes 393224 | tf_op jit(solution)/shard_map/while/body/eval_jaxpr/ppermute | solution.py:10
  321.5 80.4 %collective-permute-start = (bf16[1024,64]{1,0:T(8,128)(2,1)S(1)}, bf16[1024,64]{1,0:T(8,128)(2,1)}, u32[]{:S(2)}, u32[]{:S(2)}) collective-permute-start(bf16[1024,64]{1,0:T(8,128)(2,1)S(1)} %copy.18), channel_id=1, source_target_pairs={{8,0},{16,8},{24,16},{32,24},{40,32},{48,40},{56,48},{64,56},{72,6... | collective-permute-start | bytes 393224 | tf_op jit(solution)/shard_map/while/body/eval_jaxpr/ppermute | solution.py:10
  405.2 80.4 %collective-permute-start = (bf16[1024,64]{1,0:T(8,128)(2,1)S(1)}, bf16[1024,64]{1,0:T(8,128)(2,1)}, u32[]{:S(2)}, u32[]{:S(2)}) collective-permute-start(bf16[1024,64]{1,0:T(8,128)(2,1)S(1)} %copy.18), channel_id=1, source_target_pairs={{8,0},{16,8},{24,16},{32,24},{40,32},{48,40},{56,48},{64,56},{72,6... | collective-permute-start | bytes 393224 | tf_op jit(solution)/shard_map/while/body/eval_jaxpr/ppermute | solution.py:10
  489.0 80.4 %collective-permute-start = (bf16[1024,64]{1,0:T(8,128)(2,1)S(1)}, bf16[1024,64]{1,0:T(8,128)(2,1)}, u32[]{:S(2)}, u32[]{:S(2)}) collective-permute-start(bf16[1024,64]{1,0:T(8,128)(2,1)S(1)} %copy.18), channel_id=1, source_target_pairs={{8,0},{16,8},{24,16},{32,24},{40,32},{48,40},{56,48},{64,56},{72,6... | collective-permute-start | bytes 393224 | tf_op jit(solution)/shard_map/while/body/eval_jaxpr/ppermute | solution.py:10
  569.5 79.8 %all-reduce.5.cloned.1.call-start = ((), (), s32[]{:S(2)}) async-start(), calls=%async_computation.1 | async-start | bytes 262144 | tf_op jit(solution)/shard_map/while/body/eval_jaxpr/psum | solution.py:15
  572.8 80.7 %collective-permute-start = (bf16[1024,64]{1,0:T(8,128)(2,1)S(1)}, bf16[1024,64]{1,0:T(8,128)(2,1)}, u32[]{:S(2)}, u32[]{:S(2)}) collective-permute-start(bf16[1024,64]{1,0:T(8,128)(2,1)S(1)} %copy.18), channel_id=1, source_target_pairs={{8,0},{16,8},{24,16},{32,24},{40,32},{48,40},{56,48},{64,56},{72,6... | collective-permute-start | bytes 393224 | tf_op jit(solution)/shard_map/while/body/eval_jaxpr/ppermute | solution.py:10
  653.6 79.8 %all-reduce.5.cloned.1.call-start = ((), (), s32[]{:S(2)}) async-start(), calls=%async_computation.1 | async-start | bytes 262144 | tf_op jit(solution)/shard_map/while/body/eval_jaxpr/psum | solution.py:15
  656.9 80.7 %collective-permute-start = (bf16[1024,64]{1,0:T(8,128)(2,1)S(1)}, bf16[1024,64]{1,0:T(8,128)(2,1)}, u32[]{:S(2)}, u32[]{:S(2)}) collective-permute-start(bf16[1024,64]{1,0:T(8,128)(2,1)S(1)} %copy.18), channel_id=1, source_target_pairs={{8,0},{16,8},{24,16},{32,24},{40,32},{48,40},{56,48},{64,56},{72,6... | collective-permute-start | bytes 393224 | tf_op jit(solution)/shard_map/while/body/eval_jaxpr/ppermute | solution.py:10
  737.7 79.8 %all-reduce.5.cloned.1.call-start = ((), (), s32[]{:S(2)}) async-start(), calls=%async_computation.1 | async-start | bytes 262144 | tf_op jit(solution)/shard_map/while/body/eval_jaxpr/psum | solution.py:15
  741.0 80.7 %collective-permute-start = (bf16[1024,64]{1,0:T(8,128)(2,1)S(1)}, bf16[1024,64]{1,0:T(8,128)(2,1)}, u32[]{:S(2)}, u32[]{:S(2)}) collective-permute-start(bf16[1024,64]{1,0:T(8,128)(2,1)S(1)} %copy.18), channel_id=1, source_target_pairs={{8,0},{16,8},{24,16},{32,24},{40,32},{48,40},{56,48},{64,56},{72,6... | collective-permute-start | bytes 393224 | tf_op jit(solution)/shard_map/while/body/eval_jaxpr/ppermute | solution.py:10
  825.1 80.5 %collective-permute-start = (bf16[1024,64]{1,0:T(8,128)(2,1)S(1)}, bf16[1024,64]{1,0:T(8,128)(2,1)}, u32[]{:S(2)}, u32[]{:S(2)}) collective-permute-start(bf16[1024,64]{1,0:T(8,128)(2,1)S(1)} %copy.18), channel_id=1, source_target_pairs={{8,0},{16,8},{24,16},{32,24},{40,32},{48,40},{56,48},{64,56},{72,6... | collective-permute-start | bytes 393224 | tf_op jit(solution)/shard_map/while/body/eval_jaxpr/ppermute | solution.py:10
  905.6 79.8 %all-reduce.5.cloned.1.call-start = ((), (), s32[]{:S(2)}) async-start(), calls=%async_computation.1 | async-start | bytes 262144 | tf_op jit(solution)/shard_map/while/body/eval_jaxpr/psum | solution.py:15
  908.9 80.7 %collective-permute-start = (bf16[1024,64]{1,0:T(8,128)(2,1)S(1)}, bf16[1024,64]{1,0:T(8,128)(2,1)}, u32[]{:S(2)}, u32[]{:S(2)}) collective-permute-start(bf16[1024,64]{1,0:T(8,128)(2,1)S(1)} %copy.18), channel_id=1, source_target_pairs={{8,0},{16,8},{24,16},{32,24},{40,32},{48,40},{56,48},{64,56},{72,6... | collective-permute-start | bytes 393224 | tf_op jit(solution)/shard_map/while/body/eval_jaxpr/ppermute | solution.py:10
  993.0 80.4 %collective-permute-start = (bf16[1024,64]{1,0:T(8,128)(2,1)S(1)}, bf16[1024,64]{1,0:T(8,128)(2,1)}, u32[]{:S(2)}, u32[]{:S(2)}) collective-permute-start(bf16[1024,64]{1,0:T(8,128)(2,1)S(1)} %copy.18), channel_id=1, source_target_pairs={{8,0},{16,8},{24,16},{32,24},{40,32},{48,40},{56,48},{64,56},{72,6... | collective-permute-start | bytes 393224 | tf_op jit(solution)/shard_map/while/body/eval_jaxpr/ppermute | solution.py:10
  1073.5 79.8 %all-reduce.5.cloned.1.call-start = ((), (), s32[]{:S(2)}) async-start(), calls=%async_computation.1 | async-start | bytes 262144 | tf_op jit(solution)/shard_map/while/body/eval_jaxpr/psum | solution.py:15
  1076.8 80.7 %collective-permute-start = (bf16[1024,64]{1,0:T(8,128)(2,1)S(1)}, bf16[1024,64]{1,0:T(8,128)(2,1)}, u32[]{:S(2)}, u32[]{:S(2)}) collective-permute-start(bf16[1024,64]{1,0:T(8,128)(2,1)S(1)} %copy.18), channel_id=1, source_target_pairs={{8,0},{16,8},{24,16},{32,24},{40,32},{48,40},{56,48},{64,56},{72,6... | collective-permute-start | bytes 393224 | tf_op jit(solution)/shard_map/while/body/eval_jaxpr/ppermute | solution.py:10
  1160.9 80.4 %collective-permute-start = (bf16[1024,64]{1,0:T(8,128)(2,1)S(1)}, bf16[1024,64]{1,0:T(8,128)(2,1)}, u32[]{:S(2)}, u32[]{:S(2)}) collective-permute-start(bf16[1024,64]{1,0:T(8,128)(2,1)S(1)} %copy.18), channel_id=1, source_target_pairs={{8,0},{16,8},{24,16},{32,24},{40,32},{48,40},{56,48},{64,56},{72,6... | collective-permute-start | bytes 393224 | tf_op jit(solution)/shard_map/while/body/eval_jaxpr/ppermute | solution.py:10
  1244.7 80.5 %collective-permute-start = (bf16[1024,64]{1,0:T(8,128)(2,1)S(1)}, bf16[1024,64]{1,0:T(8,128)(2,1)}, u32[]{:S(2)}, u32[]{:S(2)}) collective-permute-start(bf16[1024,64]{1,0:T(8,128)(2,1)S(1)} %copy.18), channel_id=1, source_target_pairs={{8,0},{16,8},{24,16},{32,24},{40,32},{48,40},{56,48},{64,56},{72,6... | collective-permute-start | bytes 393224 | tf_op jit(solution)/shard_map/while/body/eval_jaxpr/ppermute | solution.py:10
  1328.6 80.4 %collective-permute-start = (bf16[1024,64]{1,0:T(8,128)(2,1)S(1)}, bf16[1024,64]{1,0:T(8,128)(2,1)}, u32[]{:S(2)}, u32[]{:S(2)}) collective-permute-start(bf16[1024,64]{1,0:T(8,128)(2,1)S(1)} %copy.18), channel_id=1, source_target_pairs={{8,0},{16,8},{24,16},{32,24},{40,32},{48,40},{56,48},{64,56},{72,6... | collective-permute-start | bytes 393224 | tf_op jit(solution)/shard_map/while/body/eval_jaxpr/ppermute | solution.py:10
  (32 other events, 2003.0 us)
Sparse Core Ops, SparseCore 0:
  66.7 78.7 all-reduce.4
  153.8 75.8 all-reduce.4
  237.9 75.8 all-reduce.4
  321.8 75.7 all-reduce.4
  405.6 75.7 all-reduce.4
  489.4 75.7 all-reduce.4
  573.5 75.7 all-reduce.4
  657.6 75.7 all-reduce.4
  741.6 75.7 all-reduce.4
  825.4 75.8 all-reduce.4
  909.6 75.7 all-reduce.4
  993.4 75.7 all-reduce.4
  1077.5 75.7 all-reduce.4
  1161.3 75.7 all-reduce.4
  1245.0 75.8 all-reduce.4
  1328.9 75.7 all-reduce.4
Sparse Core Ops, SparseCore 1:
  1412.4 75.5 all-reduce.2
where the time goes:
time: 1530 us
  waiting for transfers between devices  1130 us (74%)
  starting transfers between devices  157 us (10%)
  matrix products  69.7 us (5%)
  blocking collectives  59.5 us (4%)
  other arithmetic  57.7 us (4%)
  local copies, waits for them, and re-layouts  36 us (2%)
  between operations  16.6 us (1%)
    psum x17, waiting for transfers between devices, evaluate(): summed = lax.psum(partial_value, 'tensor')  1120 us
    ppermute x34, starting transfers between devices, from_behind(): return lax.ppermute(block, axis, route)  156 us
    another operation x33, other arithmetic  42.9 us
    dot_general x17, matrix products, evaluate(): jnp.dot(valid_act, down_piece, preferred_element_type=jnp.float32)  39.4 us
    psum x1, blocking collectives, on_device(): proj = lax.psum(partial_value, 'tensor').astype(jnp.bfloat16)  32 us
  transfers between devices with their start and end apart: 51, of which 18 were waited for; matrix products, arithmetic and copies ran while one was open for 6% of the time, Pallas kernels for 0%

commit v1 on v0

--- a/solution.py
+++ b/solution.py
@@ -2,6 +2,11 @@
 import jax.numpy as jnp
 from jax import lax
 from jax.sharding import PartitionSpec as P
+
+
+def gather_and_add(shard, axis):
+    parts = lax.all_gather(shard, axis)
+    return jnp.sum(parts, axis=0)
 
 
 def from_behind(block, axis, distance):
@@ -34,7 +39,7 @@
     train_cot = jnp.take(stored_output_gradient[0], chosen, axis=0)
     local_down_factor = adapter_down_init[0]
     partial_value = jnp.dot(train_act, local_down_factor, preferred_element_type=jnp.float32)
-    proj = lax.psum(partial_value, "tensor").astype(jnp.bfloat16)
+    proj = gather_and_add(partial_value, "tensor").astype(jnp.bfloat16)
     product = lax.dot_general(
         proj, train_cot, (((0,), (0,)), ((), ())), preferred_element_type=jnp.float32
     )

time: 1530 us -> 1520 us (level)
    psum x1 -> x0, blocking collectives: 32 us -> none  [on_device(): proj = lax.psum(partial_value, 'tensor').astype(jnp.bfloat16)]
    all_gather x0 -> x1, blocking collectives: none -> 17.9 us  [gather_and_add(): parts = lax.all_gather(shard, axis)]
where the time goes in v1:
time: 1520 us
  waiting for transfers between devices  1130 us (74%)
  starting transfers between devices  157 us (10%)
  matrix products  69.9 us (5%)
  other arithmetic  57.9 us (4%)
  blocking collectives  45.4 us (3%)
  local copies, waits for them, and re-layouts  36.2 us (2%)
  between operations  16.6 us (1%)
    psum x17, waiting for transfers between devices, evaluate(): summed = lax.psum(partial_value, 'tensor')  1120 us
    ppermute x34, starting transfers between devices, from_behind(): return lax.ppermute(block, axis, route)  156 us
    another operation x33, other arithmetic  42.9 us
    dot_general x17, matrix products, evaluate(): jnp.dot(valid_act, down_piece, preferred_element_type=jnp.float32)  39.4 us
  transfers between devices with their start and end apart: 51, of which 18 were waited for; matrix products, arithmetic and copies ran while one was open for 6% of the time, Pallas kernels for 0%

profile of v1, /device:TPU:2, one launch (start us, length us, event | category | flops | bytes accessed | tf_op | source)
XLA Modules:
  0.0 1517.2 jit_solution(3457675725591555926)
XLA Ops:
  12.5 17.9 %all-gather = f32[2048,64]{0,1:T(8,128)S(1)} all-gather(f32[256,64]{0,1:T(8,128)S(1)} %fusion.4), channel_id=2, replica_groups=mesh['skill'=64,'tensor'=8] {'tensor'}, dimensions={0}, use_global_device_ids=true | all-gather | bytes 589824 | tf_op jit(solution)/shard_map/all_gather | solution.py:8
  42.2 10.6 collective-permute-done.2
  52.8 1345.8 %while.19 = (s32[]{:T(128)}, bf16[1024,64]{1,0:T(8,128)(2,1)}, bf16[64,1920]{1,0:T(8,128)(2,1)}, f32[17,2]{1,0:T(8,128)S(1)}, bf16[512,1024]{1,0:T(8,128)(2,1)},...) while((s32[]{:T(128)}, bf16[1024,64]{1,0:T(8,128)(2,1)}, ...), condition=%wide.region_7.8_spmd, body=%wide.region_1.7_spmd.sunk | while | flops 193037824 | bytes 6709567 | solution.py:68
  56.2 11.7 collective-permute-start
  72.0 63.2 %all-reduce.5.cloned.1.call-done = f32[512,64]{0,1:T(8,128)} async-done(((f32[512,64]{0,1:T(8,128)}), f32[512,64]{0,1:T(8,128)}) %all-reduce.5.cloned.1.call-update) | async-done | bytes 131088 | tf_op jit(solution)/shard_map/while/body/eval_jaxpr/psum | solution.py:20
  142.8 5.9 collective-permute-start
  153.4 65.8 %all-reduce.5.cloned.1.call-done = f32[512,64]{0,1:T(8,128)} async-done(((f32[512,64]{0,1:T(8,128)}), f32[512,64]{0,1:T(8,128)}) %all-reduce.5.cloned.1.call-update) | async-done | bytes 131088 | tf_op jit(solution)/shard_map/while/body/eval_jaxpr/psum | solution.py:20
  226.9 5.9 collective-permute-start
  237.5 65.9 %all-reduce.5.cloned.1.call-done = f32[512,64]{0,1:T(8,128)} async-done(((f32[512,64]{0,1:T(8,128)}), f32[512,64]{0,1:T(8,128)}) %all-reduce.5.cloned.1.call-update) | async-done | bytes 131088 | tf_op jit(solution)/shard_map/while/body/eval_jaxpr/psum | solution.py:20
  321.7 65.5 %all-reduce.5.cloned.1.call-done = f32[512,64]{0,1:T(8,128)} async-done(((f32[512,64]{0,1:T(8,128)}), f32[512,64]{0,1:T(8,128)}) %all-reduce.5.cloned.1.call-update) | async-done | bytes 131088 | tf_op jit(solution)/shard_map/while/body/eval_jaxpr/psum | solution.py:20
  405.5 65.5 %all-reduce.5.cloned.1.call-done = f32[512,64]{0,1:T(8,128)} async-done(((f32[512,64]{0,1:T(8,128)}), f32[512,64]{0,1:T(8,128)}) %all-reduce.5.cloned.1.call-update) | async-done | bytes 131088 | tf_op jit(solution)/shard_map/while/body/eval_jaxpr/psum | solution.py:20
  489.3 65.5 %all-reduce.5.cloned.1.call-done = f32[512,64]{0,1:T(8,128)} async-done(((f32[512,64]{0,1:T(8,128)}), f32[512,64]{0,1:T(8,128)}) %all-reduce.5.cloned.1.call-update) | async-done | bytes 131088 | tf_op jit(solution)/shard_map/while/body/eval_jaxpr/psum | solution.py:20
  573.1 65.8 %all-reduce.5.cloned.1.call-done = f32[512,64]{0,1:T(8,128)} async-done(((f32[512,64]{0,1:T(8,128)}), f32[512,64]{0,1:T(8,128)}) %all-reduce.5.cloned.1.call-update) | async-done | bytes 131088 | tf_op jit(solution)/shard_map/while/body/eval_jaxpr/psum | solution.py:20
  657.2 65.8 %all-reduce.5.cloned.1.call-done = f32[512,64]{0,1:T(8,128)} async-done(((f32[512,64]{0,1:T(8,128)}), f32[512,64]{0,1:T(8,128)}) %all-reduce.5.cloned.1.call-update) | async-done | bytes 131088 | tf_op jit(solution)/shard_map/while/body/eval_jaxpr/psum | solution.py:20
  741.2 65.8 %all-reduce.5.cloned.1.call-done = f32[512,64]{0,1:T(8,128)} async-done(((f32[512,64]{0,1:T(8,128)}), f32[512,64]{0,1:T(8,128)}) %all-reduce.5.cloned.1.call-update) | async-done | bytes 131088 | tf_op jit(solution)/shard_map/while/body/eval_jaxpr/psum | solution.py:20
  825.3 65.6 %all-reduce.5.cloned.1.call-done = f32[512,64]{0,1:T(8,128)} async-done(((f32[512,64]{0,1:T(8,128)}), f32[512,64]{0,1:T(8,128)}) %all-reduce.5.cloned.1.call-update) | async-done | bytes 131088 | tf_op jit(solution)/shard_map/while/body/eval_jaxpr/psum | solution.py:20
  909.2 65.8 %all-reduce.5.cloned.1.call-done = f32[512,64]{0,1:T(8,128)} async-done(((f32[512,64]{0,1:T(8,128)}), f32[512,64]{0,1:T(8,128)}) %all-reduce.5.cloned.1.call-update) | async-done | bytes 131088 | tf_op jit(solution)/shard_map/while/body/eval_jaxpr/psum | solution.py:20
  993.3 65.5 %all-reduce.5.cloned.1.call-done = f32[512,64]{0,1:T(8,128)} async-done(((f32[512,64]{0,1:T(8,128)}), f32[512,64]{0,1:T(8,128)}) %all-reduce.5.cloned.1.call-update) | async-done | bytes 131088 | tf_op jit(solution)/shard_map/while/body/eval_jaxpr/psum | solution.py:20
  1077.1 65.8 %all-reduce.5.cloned.1.call-done = f32[512,64]{0,1:T(8,128)} async-done(((f32[512,64]{0,1:T(8,128)}), f32[512,64]{0,1:T(8,128)}) %all-reduce.5.cloned.1.call-update) | async-done | bytes 131088 | tf_op jit(solution)/shard_map/while/body/eval_jaxpr/psum | solution.py:20
  1161.2 65.5 %all-reduce.5.cloned.1.call-done = f32[512,64]{0,1:T(8,128)} async-done(((f32[512,64]{0,1:T(8,128)}), f32[512,64]{0,1:T(8,128)}) %all-reduce.5.cloned.1.call-update) | async-done | bytes 131088 | tf_op jit(solution)/shard_map/while/body/eval_jaxpr/psum | solution.py:20
  1245.0 65.6 %all-reduce.5.cloned.1.call-done = f32[512,64]{0,1:T(8,128)} async-done(((f32[512,64]{0,1:T(8,128)}), f32[512,64]{0,1:T(8,128)}) %all-reduce.5.cloned.1.call-update) | async-done | bytes 131088 | tf_op jit(solution)/shard_map/while/body/eval_jaxpr/psum | solution.py:20
  1328.8 65.5 %all-reduce.5.cloned.1.call-done = f32[512,64]{0,1:T(8,128)} async-done(((f32[512,64]{0,1:T(8,128)}), f32[512,64]{0,1:T(8,128)}) %all-reduce.5.cloned.1.call-update) | async-done | bytes 131088 | tf_op jit(solution)/shard_map/while/body/eval_jaxpr/psum | solution.py:20
  1402.7 74.8 %all-reduce.3.cloned.1.call-done = f32[512,64]{0,1:T(8,128)} async-done(((f32[512,64]{0,1:T(8,128)}), f32[512,64]{0,1:T(8,128)}) %all-reduce.3.cloned.1.call-update) | async-done | bytes 131088 | tf_op jit(solution)/shard_map/psum | solution.py:20
  1480.5 27.6 %psum.26 = f32[17,2]{1,0:T(8,128)S(1)} all-reduce(f32[17,2]{1,0:T(8,128)S(1)} %scatter.7), channel_id=1, replica_groups=mesh['skill'=64,'tensor'=8] {'tensor'}, use_global_device_ids=true, to_apply=%region_12.13 | all-reduce | flops 34 | bytes 272 | tf_op jit(solution)/shard_map/psum | solution.py:72
  (257 shorter events, 297.7 us)
Async XLA Ops:
  52.8 82.3 %all-reduce.5.cloned.1.call-start = ((), (), s32[]{:S(2)}) async-start(), calls=%async_computation.1 | async-start | bytes 262144 | tf_op jit(solution)/shard_map/while/body/eval_jaxpr/psum | solution.py:20
  56.2 83.3 %collective-permute-start = (bf16[1024,64]{1,0:T(8,128)(2,1)S(1)}, bf16[1024,64]{1,0:T(8,128)(2,1)}, u32[]{:S(2)}, u32[]{:S(2)}) collective-permute-start(bf16[1024,64]{1,0:T(8,128)(2,1)S(1)} %copy.20), channel_id=1, source_target_pairs={{8,0},{16,8},{24,16},{32,24},{40,32},{48,40},{56,48},{64,56},{72,6... | collective-permute-start | bytes 393224 | tf_op jit(solution)/shard_map/while/body/eval_jaxpr/ppermute | solution.py:15
  139.4 79.8 %all-reduce.5.cloned.1.call-start = ((), (), s32[]{:S(2)}) async-start(), calls=%async_computation.1 | async-start | bytes 262144 | tf_op jit(solution)/shard_map/while/body/eval_jaxpr/psum | solution.py:20
  142.8 80.7 %collective-permute-start = (bf16[1024,64]{1,0:T(8,128)(2,1)S(1)}, bf16[1024,64]{1,0:T(8,128)(2,1)}, u32[]{:S(2)}, u32[]{:S(2)}) collective-permute-start(bf16[1024,64]{1,0:T(8,128)(2,1)S(1)} %copy.20), channel_id=1, source_target_pairs={{8,0},{16,8},{24,16},{32,24},{40,32},{48,40},{56,48},{64,56},{72,6... | collective-permute-start | bytes 393224 | tf_op jit(solution)/shard_map/while/body/eval_jaxpr/ppermute | solution.py:15
  223.5 79.9 %all-reduce.5.cloned.1.call-start = ((), (), s32[]{:S(2)}) async-start(), calls=%async_computation.1 | async-start | bytes 262144 | tf_op jit(solution)/shard_map/while/body/eval_jaxpr/psum | solution.py:20
  226.9 80.8 %collective-permute-start = (bf16[1024,64]{1,0:T(8,128)(2,1)S(1)}, bf16[1024,64]{1,0:T(8,128)(2,1)}, u32[]{:S(2)}, u32[]{:S(2)}) collective-permute-start(bf16[1024,64]{1,0:T(8,128)(2,1)S(1)} %copy.20), channel_id=1, source_target_pairs={{8,0},{16,8},{24,16},{32,24},{40,32},{48,40},{56,48},{64,56},{72,6... | collective-permute-start | bytes 393224 | tf_op jit(solution)/shard_map/while/body/eval_jaxpr/ppermute | solution.py:15
  311.0 80.4 %collective-permute-start = (bf16[1024,64]{1,0:T(8,128)(2,1)S(1)}, bf16[1024,64]{1,0:T(8,128)(2,1)}, u32[]{:S(2)}, u32[]{:S(2)}) collective-permute-start(bf16[1024,64]{1,0:T(8,128)(2,1)S(1)} %copy.20), channel_id=1, source_target_pairs={{8,0},{16,8},{24,16},{32,24},{40,32},{48,40},{56,48},{64,56},{72,6... | collective-permute-start | bytes 393224 | tf_op jit(solution)/shard_map/while/body/eval_jaxpr/ppermute | solution.py:15
  394.8 80.4 %collective-permute-start = (bf16[1024,64]{1,0:T(8,128)(2,1)S(1)}, bf16[1024,64]{1,0:T(8,128)(2,1)}, u32[]{:S(2)}, u32[]{:S(2)}) collective-permute-start(bf16[1024,64]{1,0:T(8,128)(2,1)S(1)} %copy.20), channel_id=1, source_target_pairs={{8,0},{16,8},{24,16},{32,24},{40,32},{48,40},{56,48},{64,56},{72,6... | collective-permute-start | bytes 393224 | tf_op jit(solution)/shard_map/while/body/eval_jaxpr/ppermute | solution.py:15
  478.6 80.4 %collective-permute-start = (bf16[1024,64]{1,0:T(8,128)(2,1)S(1)}, bf16[1024,64]{1,0:T(8,128)(2,1)}, u32[]{:S(2)}, u32[]{:S(2)}) collective-permute-start(bf16[1024,64]{1,0:T(8,128)(2,1)S(1)} %copy.20), channel_id=1, source_target_pairs={{8,0},{16,8},{24,16},{32,24},{40,32},{48,40},{56,48},{64,56},{72,6... | collective-permute-start | bytes 393224 | tf_op jit(solution)/shard_map/while/body/eval_jaxpr/ppermute | solution.py:15
  559.1 79.8 %all-reduce.5.cloned.1.call-start = ((), (), s32[]{:S(2)}) async-start(), calls=%async_computation.1 | async-start | bytes 262144 | tf_op jit(solution)/shard_map/while/body/eval_jaxpr/psum | solution.py:20
  562.4 80.7 %collective-permute-start = (bf16[1024,64]{1,0:T(8,128)(2,1)S(1)}, bf16[1024,64]{1,0:T(8,128)(2,1)}, u32[]{:S(2)}, u32[]{:S(2)}) collective-permute-start(bf16[1024,64]{1,0:T(8,128)(2,1)S(1)} %copy.20), channel_id=1, source_target_pairs={{8,0},{16,8},{24,16},{32,24},{40,32},{48,40},{56,48},{64,56},{72,6... | collective-permute-start | bytes 393224 | tf_op jit(solution)/shard_map/while/body/eval_jaxpr/ppermute | solution.py:15
  643.1 79.8 %all-reduce.5.cloned.1.call-start = ((), (), s32[]{:S(2)}) async-start(), calls=%async_computation.1 | async-start | bytes 262144 | tf_op jit(solution)/shard_map/while/body/eval_jaxpr/psum | solution.py:20
  646.5 80.7 %collective-permute-start = (bf16[1024,64]{1,0:T(8,128)(2,1)S(1)}, bf16[1024,64]{1,0:T(8,128)(2,1)}, u32[]{:S(2)}, u32[]{:S(2)}) collective-permute-start(bf16[1024,64]{1,0:T(8,128)(2,1)S(1)} %copy.20), channel_id=1, source_target_pairs={{8,0},{16,8},{24,16},{32,24},{40,32},{48,40},{56,48},{64,56},{72,6... | collective-permute-start | bytes 393224 | tf_op jit(solution)/shard_map/while/body/eval_jaxpr/ppermute | solution.py:15
  727.2 79.8 %all-reduce.5.cloned.1.call-start = ((), (), s32[]{:S(2)}) async-start(), calls=%async_computation.1 | async-start | bytes 262144 | tf_op jit(solution)/shard_map/while/body/eval_jaxpr/psum | solution.py:20
  730.6 80.7 %collective-permute-start = (bf16[1024,64]{1,0:T(8,128)(2,1)S(1)}, bf16[1024,64]{1,0:T(8,128)(2,1)}, u32[]{:S(2)}, u32[]{:S(2)}) collective-permute-start(bf16[1024,64]{1,0:T(8,128)(2,1)S(1)} %copy.20), channel_id=1, source_target_pairs={{8,0},{16,8},{24,16},{32,24},{40,32},{48,40},{56,48},{64,56},{72,6... | collective-permute-start | bytes 393224 | tf_op jit(solution)/shard_map/while/body/eval_jaxpr/ppermute | solution.py:15
  814.7 80.5 %collective-permute-start = (bf16[1024,64]{1,0:T(8,128)(2,1)S(1)}, bf16[1024,64]{1,0:T(8,128)(2,1)}, u32[]{:S(2)}, u32[]{:S(2)}) collective-permute-start(bf16[1024,64]{1,0:T(8,128)(2,1)S(1)} %copy.20), channel_id=1, source_target_pairs={{8,0},{16,8},{24,16},{32,24},{40,32},{48,40},{56,48},{64,56},{72,6... | collective-permute-start | bytes 393224 | tf_op jit(solution)/shard_map/while/body/eval_jaxpr/ppermute | solution.py:15
  895.2 79.8 %all-reduce.5.cloned.1.call-start = ((), (), s32[]{:S(2)}) async-start(), calls=%async_computation.1 | async-start | bytes 262144 | tf_op jit(solution)/shard_map/while/body/eval_jaxpr/psum | solution.py:20
  898.5 80.7 %collective-permute-start = (bf16[1024,64]{1,0:T(8,128)(2,1)S(1)}, bf16[1024,64]{1,0:T(8,128)(2,1)}, u32[]{:S(2)}, u32[]{:S(2)}) collective-permute-start(bf16[1024,64]{1,0:T(8,128)(2,1)S(1)} %copy.20), channel_id=1, source_target_pairs={{8,0},{16,8},{24,16},{32,24},{40,32},{48,40},{56,48},{64,56},{72,6... | collective-permute-start | bytes 393224 | tf_op jit(solution)/shard_map/while/body/eval_jaxpr/ppermute | solution.py:15
  982.6 80.4 %collective-permute-start = (bf16[1024,64]{1,0:T(8,128)(2,1)S(1)}, bf16[1024,64]{1,0:T(8,128)(2,1)}, u32[]{:S(2)}, u32[]{:S(2)}) collective-permute-start(bf16[1024,64]{1,0:T(8,128)(2,1)S(1)} %copy.20), channel_id=1, source_target_pairs={{8,0},{16,8},{24,16},{32,24},{40,32},{48,40},{56,48},{64,56},{72,6... | collective-permute-start | bytes 393224 | tf_op jit(solution)/shard_map/while/body/eval_jaxpr/ppermute | solution.py:15
  1063.1 79.8 %all-reduce.5.cloned.1.call-start = ((), (), s32[]{:S(2)}) async-start(), calls=%async_computation.1 | async-start | bytes 262144 | tf_op jit(solution)/shard_map/while/body/eval_jaxpr/psum | solution.py:20
  1066.4 80.7 %collective-permute-start = (bf16[1024,64]{1,0:T(8,128)(2,1)S(1)}, bf16[1024,64]{1,0:T(8,128)(2,1)}, u32[]{:S(2)}, u32[]{:S(2)}) collective-permute-start(bf16[1024,64]{1,0:T(8,128)(2,1)S(1)} %copy.20), channel_id=1, source_target_pairs={{8,0},{16,8},{24,16},{32,24},{40,32},{48,40},{56,48},{64,56},{72,6... | collective-permute-start | bytes 393224 | tf_op jit(solution)/shard_map/while/body/eval_jaxpr/ppermute | solution.py:15
  1150.5 80.4 %collective-permute-start = (bf16[1024,64]{1,0:T(8,128)(2,1)S(1)}, bf16[1024,64]{1,0:T(8,128)(2,1)}, u32[]{:S(2)}, u32[]{:S(2)}) collective-permute-start(bf16[1024,64]{1,0:T(8,128)(2,1)S(1)} %copy.20), channel_id=1, source_target_pairs={{8,0},{16,8},{24,16},{32,24},{40,32},{48,40},{56,48},{64,56},{72,6... | collective-permute-start | bytes 393224 | tf_op jit(solution)/shard_map/while/body/eval_jaxpr/ppermute | solution.py:15
  1234.3 80.5 %collective-permute-start = (bf16[1024,64]{1,0:T(8,128)(2,1)S(1)}, bf16[1024,64]{1,0:T(8,128)(2,1)}, u32[]{:S(2)}, u32[]{:S(2)}) collective-permute-start(bf16[1024,64]{1,0:T(8,128)(2,1)S(1)} %copy.20), channel_id=1, source_target_pairs={{8,0},{16,8},{24,16},{32,24},{40,32},{48,40},{56,48},{64,56},{72,6... | collective-permute-start | bytes 393224 | tf_op jit(solution)/shard_map/while/body/eval_jaxpr/ppermute | solution.py:15
  1318.1 80.4 %collective-permute-start = (bf16[1024,64]{1,0:T(8,128)(2,1)S(1)}, bf16[1024,64]{1,0:T(8,128)(2,1)}, u32[]{:S(2)}, u32[]{:S(2)}) collective-permute-start(bf16[1024,64]{1,0:T(8,128)(2,1)S(1)} %copy.20), channel_id=1, source_target_pairs={{8,0},{16,8},{24,16},{32,24},{40,32},{48,40},{56,48},{64,56},{72,6... | collective-permute-start | bytes 393224 | tf_op jit(solution)/shard_map/while/body/eval_jaxpr/ppermute | solution.py:15
  (32 other events, 1997.4 us)
Sparse Core Ops, SparseCore 0:
  56.8 78.2 all-reduce.4
  143.4 75.7 all-reduce.4
  227.5 75.8 all-reduce.4
  311.4 75.7 all-reduce.4
  395.2 75.7 all-reduce.4
  479.0 75.7 all-reduce.4
  563.0 75.7 all-reduce.4
  647.1 75.7 all-reduce.4
  731.2 75.7 all-reduce.4
  815.0 75.8 all-reduce.4
  899.2 75.7 all-reduce.4
  983.0 75.7 all-reduce.4
  1067.1 75.7 all-reduce.4
  1150.8 75.7 all-reduce.4
  1234.6 75.8 all-reduce.4
  1318.5 75.7 all-reduce.4
Sparse Core Ops, SparseCore 1:
  1402.0 75.5 all-reduce.2
